TPU v7x, 32 devices: a whole 2x2x4 slice. The times are simulated.
32 devices in a mesh: groups: 2 (over x), port: 16 (over z, y, core).
Axes of the slice: x: 2, y: 2, z: 4, core: 2. Of those that a mesh axis runs over, the one named last changes fastest.
Arguments:
- measured: bfloat16 [4, 2, 4096, 4096], P('groups', None, 'port'), parts along dimension 0, may hold values from -6 to 6
- out_factor: bfloat16 [4096, 1024], P('port', 'groups'), parts along dimension 1, may hold values from -0.25 to 0.25
- in_factor: bfloat16 [1024, 4096], P('groups', 'port'), parts along dimension 0, may hold values from -6 to 6
- pole_rates: float32 [1024], P('groups'), parts along dimension 0, may hold values from 0.1 to 10
- freq_index: int32 [4], P('groups'), parts along dimension 0, may hold values from 0 to 1023
- quad_codes: int32 [4], P('groups'), parts along dimension 0, may hold values from 1 to 4
Outputs:
- grad_out: float32 [4096, 1024], P('port', 'groups'), parts along dimension 1
- grad_in_t: float32 [4096, 1024], P('port', 'groups'), parts along dimension 1
There are 2 independent parts, one for each index of `groups`. A program takes and returns all parts, laid end to end along the dimension named above; each array names one. Nothing has to cross between parts.
All inputs are finite; a program needn't handle non-finite values.
Results may differ from a plain program's by a relative error of at most 0.002.
Values may be sent and summed in bfloat16 or wider, within the bound.
A program may use at most 64 MiB of HBM per device.

v0:
```python
import math
import jax
import jax.numpy as jnp
from jax import lax
from jax.sharding import PartitionSpec as P

GRID = 1024
low_freq = 0.1
log_span = math.log(100.0)


def pole_terms(freq_index, pole_rates):
    omega = low_freq * jnp.exp(log_span * freq_index.astype(jnp.float32) / (GRID - 1))
    denominator = pole_rates[None, :] * pole_rates[None, :] + omega[:, None] * omega[:, None]
    real_side = pole_rates[None, :] / denominator
    imag_side = -omega[:, None] / denominator
    return jnp.stack([real_side, imag_side], axis=1)


def contract_first(left, right):
    return lax.dot_general(
        left, right, (((0,), (0,)), ((), ())), preferred_element_type=jnp.float32
    )


def contract_second(left, right):
    return lax.dot_general(
        left, right, (((1,), (1,)), ((), ())), preferred_element_type=jnp.float32
    )


def on_device(measured, out_factor, in_factor, pole_rates, freq_index, quad_codes):
    freq_count = measured.shape[0]
    local_rows = out_factor.shape[0]
    pole_count = out_factor.shape[1]
    local_cols = in_factor.shape[1]
    total_in = measured.shape[3]
    total_out = local_rows * lax.axis_size("port")
    coefficients = pole_terms(freq_index, pole_rates)
    weights = quad_codes.astype(jnp.float32) * 0.25
    weighted = weights[:, None, None] * coefficients
    scaled = (
        out_factor.astype(jnp.float32)[None, None, :, :] * coefficients[:, :, None, :]
    ).astype(jnp.bfloat16)
    block_cols = lax.all_gather(in_factor, "port", axis=1, tiled=True)
    width_cols = block_cols.shape[1]
    model = jnp.dot(scaled.reshape(-1, pole_count), block_cols, preferred_element_type=jnp.float32)
    model = model.reshape(freq_count, 2, local_rows, width_cols)
    residual = (model - measured.astype(jnp.float32)).astype(jnp.bfloat16)
    update = contract_second(residual.reshape(-1, width_cols), block_cols)
    update = update.reshape(freq_count, 2, local_rows, pole_count)
    grad_out = jnp.zeros((local_rows, pole_count), jnp.float32)
    for freq_slot in range(freq_count):
        for comp_slot in range(2):
            grad_out = (
                grad_out + weighted[freq_slot, comp_slot][None, :] * update[freq_slot, comp_slot]
            )
    grad_out = grad_out * (1.0 / math.sqrt(total_in))
    running = jnp.zeros((local_cols * lax.axis_size("port"), pole_count), jnp.float32)
    for freq_slot in range(freq_count):
        for comp_slot in range(2):
            running = running + weighted[freq_slot, comp_slot][None, :] * contract_first(
                residual[freq_slot, comp_slot], out_factor
            )
    grad_in_t = lax.psum_scatter(running, "port", scatter_dimension=0, tiled=True)
    grad_in_t = grad_in_t * (1.0 / math.sqrt(total_out))
    return (grad_out, grad_in_t)


def solution(mesh):
    in_specs = (
        P("groups", None, "port", None),
        P("port", "groups"),
        P("groups", "port"),
        P("groups"),
        P("groups"),
        P("groups"),
    )
    out_specs = (P("port", "groups"), P("port", "groups"))
    return jax.shard_map(
        on_device, mesh=mesh, in_specs=in_specs, out_specs=out_specs, check_vma=False
    )
```

profile of v0, /device:TPU:0, one launch (start us, length us, event | category | flops | bytes accessed | tf_op | source)
XLA Modules:
  0.0 206.1 jit_solution(8669891354242152455)
XLA Ops:
  7.2 0.0 all-gather.2.cloned.1.call-start
  7.2 0.7 all-gather.2.cloned.1.call-update
  7.9 0.0 reduce-scatter.2.cloned.1.call-start
  7.9 0.8 mul.118
  8.7 1.0 convert_element_type.22
  9.7 0.7 convert_multiply_fusion
  10.4 0.7 fusion.17
  11.0 0.8 add_divide_fusion.1
  11.8 0.1 broadcast_multiply_fusion.1
  11.9 53.5 %all-gather.2.cloned.1.call-done = bf16[512,4096]{1,0:T(8,128)(2,1)} async-done(((bf16[512,256]{1,0:T(8,128)(2,1)}), bf16[512,4096]{1,0:T(8,128)(2,1)}) %all-gather.2.cloned.1.call-update) | async-done | bytes 4194320 | tf_op jit(solution)/shard_map/all_gather | solution.py:45
  65.4 0.0 copy-start.1
  65.4 8.3 %subtract_convert_fusion = bf16[2,2,256,4096]{3,2,1,0:T(8,128)(2,1)S(1)} fusion(bf16[2,2,256,4096]{3,2,1,0:T(8,128)(2,1)} %param.6, bf16[512,4096]{1,0:T(8,128)(2,1)} %all-gather.2.cloned.1.call-done, f32[2,2,512]{2,1,0:T(2,128)S(1)} %get-tuple-element.7, f32[256,512]{1,0:T(8,128)S(1)} %convert_element_type.22), kind=kOutput, calls=%fused_computation | convolution fusion | flops 4308598784 | bytes 21504000 | tf_op jit(solution)/shard_map/dot_general | solution.py:47
  73.6 0.0 copy-start
  73.7 3.2 %copy-done = bf16[2,2,256,4096]{3,2,1,0:T(8,128)(2,1)} copy-done((bf16[2,2,256,4096]{3,2,1,0:T(8,128)(2,1)}, bf16[2,2,256,4096]{3,2,1,0:T(8,128)(2,1)S(1)}, u32[]{:S(2)}) %copy-start) | copy-done | bytes 8388632
  76.9 0.0 copy-done.1
  76.9 1.3 fusion.3
  78.2 2.9 %fusion.4 = f32[4096,512]{1,0:T(8,128)S(1)} fusion(bf16[256,512]{1,0:T(8,128)(2,1)S(1)} %copy-done.1, bf16[2,2,256,4096]{3,2,1,0:T(8,128)(2,1)} %copy-done), kind=kOutput, calls=%fused_computation.9 | convolution fusion | flops 1073741824 | bytes 10747904 | tf_op jit(solution)/shard_map/dot_general | solution.py:21
  81.1 6.1 %fusion.5 = f32[4096,512]{1,0:T(8,128)} fusion(bf16[256,512]{1,0:T(8,128)(2,1)S(1)} %copy-done.1, bf16[2,2,256,4096]{3,2,1,0:T(8,128)(2,1)} %copy-done), kind=kOutput, calls=%fused_computation.11 | convolution fusion | flops 1073741824 | bytes 10747904 | tf_op jit(solution)/shard_map/dot_general | solution.py:21
  87.2 8.4 %multiply_add_fusion = f32[4096,512]{1,0:T(8,128)} fusion(f32[4096,512]{1,0:T(8,128)S(1)} %fusion.3, f32[4096,512]{1,0:T(8,128)S(1)} %fusion.4, f32[4096,512]{1,0:T(8,128)} %fusion.5, bf16[256,512]{1,0:T(8,128)(2,1)S(1)} %copy-done.1, f32[512]{0:T(512)S(1)} %bitcast.60, f32[512]{0:T(512)S(1)} %bitcast.62, f32[512]{0:T(512)S(1)} %bitcast.64, ...), kind=kOutput, calls=%fused_computation.1 | convolution fusion | flops 1088421888 | bytes 35921920 | tf_op jit(solution)/shard_map/dot_general | solution.py:21
  95.6 0.0 reduce-scatter.2.cloned.1.call-update
  95.6 8.2 %fusion = f32[2,2,256,512]{3,2,1,0:T(8,128)S(1)} fusion(bf16[2,2,256,4096]{3,2,1,0:T(8,128)(2,1)} %copy-done, bf16[512,4096]{1,0:T(8,128)(2,1)} %all-gather.2.cloned.1.call-done), kind=kOutput, calls=%fused_computation.2 | convolution fusion | flops 4294967296 | bytes 14680064 | tf_op jit(solution)/shard_map/dot_general | solution.py:27
  103.9 1.0 fusion.10
  104.9 92.5 %reduce-scatter.2.cloned.1.call-done = f32[256,512]{1,0:T(8,128)} async-done(((f32[4096,512]{1,0:T(8,128)}), f32[256,512]{1,0:T(8,128)}) %reduce-scatter.2.cloned.1.call-update) | async-done | bytes 524304 | tf_op jit(solution)/shard_map/reduce_scatter | solution.py:65
  197.4 1.9 broadcast_multiply_fusion
  (1 shorter events, 0.0 us)
Async XLA Ops:
  7.2 58.2 %all-gather.2.cloned.1.call-start = ((), (), s32[]{:S(2)}) async-start(), calls=%async_computation.1 | async-start | bytes 4456448 | tf_op jit(solution)/shard_map/all_gather | solution.py:45
  7.9 189.5 %reduce-scatter.2.cloned.1.call-start = ((), (), s32[]{:S(2)}) async-start(), calls=%async_computation.2 | async-start | bytes 8912896 | tf_op jit(solution)/shard_map/reduce_scatter | solution.py:65
  65.4 11.5 %copy-start.1 = (bf16[256,512]{1,0:T(8,128)(2,1)S(1)}, bf16[256,512]{1,0:T(8,128)(2,1)}, u32[]{:S(2)}) copy-start(bf16[256,512]{1,0:T(8,128)(2,1)} %param.7) | copy-start | bytes 786436
  73.6 3.2 %copy-start = (bf16[2,2,256,4096]{3,2,1,0:T(8,128)(2,1)}, bf16[2,2,256,4096]{3,2,1,0:T(8,128)(2,1)S(1)}, u32[]{:S(2)}) copy-start(bf16[2,2,256,4096]{3,2,1,0:T(8,128)(2,1)S(1)} %subtract_convert_fusion) | copy-start | bytes 25165828
Sparse Core Ops, SparseCore 0:
  10.1 55.1 all-gather.1
  95.8 101.5 reduce-scatter.1
where the time goes:
time: 206 us
  waiting for transfers between devices  147 us (71%)
  matrix products  35.2 us (17%)
  between operations  14.1 us (7%)
  other arithmetic  6.84 us (3%)
  local copies, waits for them, and re-layouts  3.23 us (2%)
    reduce_scatter x1, waiting for transfers between devices, on_device(): lax.psum_scatter(running, 'port', scatter_dimension=0, tiled=True)  92.5 us
    all_gather x1, waiting for transfers between devices, on_device(): block_cols = lax.all_gather(in_factor, 'port', axis=1, tiled=True)  53.5 us
    dot_general x4, matrix products, contract_first(): lax.dot_general(left, right, (((0,), (0,)), ((), ())), preferred_element_...  18.7 us
    dot_general x1, matrix products, on_device(): jnp.dot(scaled.reshape(-1, pole_count), block_cols, preferred_element_typ...  8.27 us
    dot_general x1, matrix products, contract_second(): lax.dot_general(left, right, (((1,), (1,)), ((), ())), preferred_element_...  8.24 us
  transfers between devices with their start and end apart: 2, of which 2 were waited for; matrix products, arithmetic and copies ran while one was open for 6% of the time, Pallas kernels for 0%

commit v1 on v0

--- a/solution.py
+++ b/solution.py
@@ -3,6 +3,7 @@
 import jax.numpy as jnp
 from jax import lax
 from jax.sharding import PartitionSpec as P
+from jax.lax import axis_index, axis_size, ppermute
 
 GRID = 1024
 low_freq = 0.1
@@ -42,7 +43,14 @@
     scaled = (
         out_factor.astype(jnp.float32)[None, None, :, :] * coefficients[:, :, None, :]
     ).astype(jnp.bfloat16)
-    block_cols = lax.all_gather(in_factor, "port", axis=1, tiled=True)
+    xs_all = [in_factor]
+    q_n = axis_size("port")
+    for tick in range(q_n - 1):
+        known = ppermute(xs_all[-1], "port", [(k0, (k0 + 1) % q_n) for k0 in range(q_n)])
+        xs_all.append(known)
+    opened = jnp.concatenate(xs_all[::-1], axis=1)
+    m_next = axis_index("port")
+    block_cols = jnp.roll(opened, shift=(m_next + 1) * in_factor.shape[1], axis=1)
     width_cols = block_cols.shape[1]
     model = jnp.dot(scaled.reshape(-1, pole_count), block_cols, preferred_element_type=jnp.float32)
     model = model.reshape(freq_count, 2, local_rows, width_cols)

time: 206 us -> 286 us (1.39)
  waiting for transfers between devices: 147 us -> 216 us
  local copies, waits for them, and re-layouts: 3.23 us -> 13.1 us
    ppermute x0 -> x15, waiting for transfers between devices: none -> 124 us  [on_device(): ppermute(xs_all[-1], 'port', [(k0, (k0 + 1) % q_n) for k0 in range(q_n)])]
    all_gather x1 -> x0, waiting for transfers between devices: 53.5 us -> none  [on_device(): block_cols = lax.all_gather(in_factor, 'port', axis=1, tiled=True)]
    unnamed x4 -> x41, local copies, waits for them, and re-layouts: 3.22 us -> 13 us
  transfers between devices with their start and end apart: 2 -> 16, of which waited for: 2 -> 16; matrix products, arithmetic and copies ran while one was open for 6% -> 5% of each run, Pallas kernels for 0% -> 0%
where the time goes in v1:
time: 286 us
  waiting for transfers between devices  216 us (76%)
  matrix products  34.3 us (12%)
  between operations  14.4 us (5%)
  local copies, waits for them, and re-layouts  13.1 us (5%)
  other arithmetic  7.63 us (3%)
    ppermute x15, waiting for transfers between devices, on_device(): ppermute(xs_all[-1], 'port', [(k0, (k0 + 1) % q_n) for k0 in range(q_n)])  124 us
    reduce_scatter x1, waiting for transfers between devices, on_device(): lax.psum_scatter(running, 'port', scatter_dimension=0, tiled=True)  91.8 us
    dot_general x4, matrix products, contract_first(): lax.dot_general(left, right, (((0,), (0,)), ((), ())), preferred_element_...  18.9 us
    unnamed x41, local copies, waits for them, and re-layouts  13 us
    dot_general x1, matrix products, contract_second(): lax.dot_general(left, right, (((1,), (1,)), ((), ())), preferred_element_...  8.42 us
    dot_general x1, matrix products, on_device(): jnp.dot(scaled.reshape(-1, pole_count), block_cols, preferred_element_typ...  7.06 us
  transfers between devices with their start and end apart: 16, of which 16 were waited for; matrix products, arithmetic and copies ran while one was open for 5% of the time, Pallas kernels for 0%

profile of v1, /device:TPU:0, one launch (start us, length us, event | category | flops | bytes accessed | tf_op | source)
XLA Modules:
  0.0 286.0 jit_solution(10098766306626322135)
XLA Ops:
  7.8 9.2 %collective-permute-done = bf16[512,256]{1,0:T(8,128)(2,1)S(1)} collective-permute-done((bf16[512,256]{1,0:T(8,128)(2,1)}, bf16[512,256]{1,0:T(8,128)(2,1)S(1)}, u32[]{:S(2)}, u32[]{:S(2)}) %collective-permute-start) | collective-permute-done | bytes 262176 | tf_op jit(solution)/shard_map/ppermute | solution.py:49
  17.0 8.5 %collective-permute-done.1 = bf16[512,256]{1,0:T(8,128)(2,1)S(1)} collective-permute-done((bf16[512,256]{1,0:T(8,128)(2,1)S(1)}, bf16[512,256]{1,0:T(8,128)(2,1)S(1)}, u32[]{:S(2)}, u32[]{:S(2)}) %collective-permute-start.1) | collective-permute-done | bytes 262176 | tf_op jit(solution)/shard_map/ppermute | solution.py:49
  25.5 8.5 %collective-permute-done.2 = bf16[512,256]{1,0:T(8,128)(2,1)S(1)} collective-permute-done((bf16[512,256]{1,0:T(8,128)(2,1)S(1)}, bf16[512,256]{1,0:T(8,128)(2,1)S(1)}, u32[]{:S(2)}, u32[]{:S(2)}) %collective-permute-start.2) | collective-permute-done | bytes 262176 | tf_op jit(solution)/shard_map/ppermute | solution.py:49
  34.0 8.5 %collective-permute-done.3 = bf16[512,256]{1,0:T(8,128)(2,1)S(1)} collective-permute-done((bf16[512,256]{1,0:T(8,128)(2,1)S(1)}, bf16[512,256]{1,0:T(8,128)(2,1)S(1)}, u32[]{:S(2)}, u32[]{:S(2)}) %collective-permute-start.3) | collective-permute-done | bytes 262176 | tf_op jit(solution)/shard_map/ppermute | solution.py:49
  42.5 8.5 %collective-permute-done.4 = bf16[512,256]{1,0:T(8,128)(2,1)S(1)} collective-permute-done((bf16[512,256]{1,0:T(8,128)(2,1)S(1)}, bf16[512,256]{1,0:T(8,128)(2,1)S(1)}, u32[]{:S(2)}, u32[]{:S(2)}) %collective-permute-start.4) | collective-permute-done | bytes 262176 | tf_op jit(solution)/shard_map/ppermute | solution.py:49
  51.0 8.5 %collective-permute-done.5 = bf16[512,256]{1,0:T(8,128)(2,1)S(1)} collective-permute-done((bf16[512,256]{1,0:T(8,128)(2,1)S(1)}, bf16[512,256]{1,0:T(8,128)(2,1)S(1)}, u32[]{:S(2)}, u32[]{:S(2)}) %collective-permute-start.5) | collective-permute-done | bytes 262176 | tf_op jit(solution)/shard_map/ppermute | solution.py:49
  59.5 8.5 %collective-permute-done.6 = bf16[512,256]{1,0:T(8,128)(2,1)S(1)} collective-permute-done((bf16[512,256]{1,0:T(8,128)(2,1)S(1)}, bf16[512,256]{1,0:T(8,128)(2,1)S(1)}, u32[]{:S(2)}, u32[]{:S(2)}) %collective-permute-start.6) | collective-permute-done | bytes 262176 | tf_op jit(solution)/shard_map/ppermute | solution.py:49
  68.0 8.5 %collective-permute-done.7 = bf16[512,256]{1,0:T(8,128)(2,1)S(1)} collective-permute-done((bf16[512,256]{1,0:T(8,128)(2,1)S(1)}, bf16[512,256]{1,0:T(8,128)(2,1)S(1)}, u32[]{:S(2)}, u32[]{:S(2)}) %collective-permute-start.7) | collective-permute-done | bytes 262176 | tf_op jit(solution)/shard_map/ppermute | solution.py:49
  76.5 8.5 %collective-permute-done.8 = bf16[512,256]{1,0:T(8,128)(2,1)S(1)} collective-permute-done((bf16[512,256]{1,0:T(8,128)(2,1)S(1)}, bf16[512,256]{1,0:T(8,128)(2,1)S(1)}, u32[]{:S(2)}, u32[]{:S(2)}) %collective-permute-start.8) | collective-permute-done | bytes 262176 | tf_op jit(solution)/shard_map/ppermute | solution.py:49
  85.0 8.5 %collective-permute-done.9 = bf16[512,256]{1,0:T(8,128)(2,1)S(1)} collective-permute-done((bf16[512,256]{1,0:T(8,128)(2,1)S(1)}, bf16[512,256]{1,0:T(8,128)(2,1)S(1)}, u32[]{:S(2)}, u32[]{:S(2)}) %collective-permute-start.9) | collective-permute-done | bytes 262176 | tf_op jit(solution)/shard_map/ppermute | solution.py:49
  93.5 8.5 %collective-permute-done.10 = bf16[512,256]{1,0:T(8,128)(2,1)S(1)} collective-permute-done((bf16[512,256]{1,0:T(8,128)(2,1)S(1)}, bf16[512,256]{1,0:T(8,128)(2,1)S(1)}, u32[]{:S(2)}, u32[]{:S(2)}) %collective-permute-start.10) | collective-permute-done | bytes 262176 | tf_op jit(solution)/shard_map/ppermute | solution.py:49
  102.0 8.5 %collective-permute-done.11 = bf16[512,256]{1,0:T(8,128)(2,1)S(1)} collective-permute-done((bf16[512,256]{1,0:T(8,128)(2,1)S(1)}, bf16[512,256]{1,0:T(8,128)(2,1)S(1)}, u32[]{:S(2)}, u32[]{:S(2)}) %collective-permute-start.11) | collective-permute-done | bytes 262176 | tf_op jit(solution)/shard_map/ppermute | solution.py:49
  111.1 7.9 %collective-permute-done.12 = bf16[512,256]{1,0:T(8,128)(2,1)} collective-permute-done((bf16[512,256]{1,0:T(8,128)(2,1)S(1)}, bf16[512,256]{1,0:T(8,128)(2,1)}, u32[]{:S(2)}, u32[]{:S(2)}) %collective-permute-start.12) | collective-permute-done | bytes 262176 | tf_op jit(solution)/shard_map/ppermute | solution.py:49
  121.2 6.6 %collective-permute-done.13 = bf16[512,256]{1,0:T(8,128)(2,1)} collective-permute-done((bf16[512,256]{1,0:T(8,128)(2,1)}, bf16[512,256]{1,0:T(8,128)(2,1)}, u32[]{:S(2)}, u32[]{:S(2)}) %collective-permute-start.13) | collective-permute-done | bytes 262176 | tf_op jit(solution)/shard_map/ppermute | solution.py:49
  127.9 1.8 convert_element_type.22
  129.8 6.9 %collective-permute-done.14 = bf16[512,256]{1,0:T(8,128)(2,1)} collective-permute-done((bf16[512,256]{1,0:T(8,128)(2,1)}, bf16[512,256]{1,0:T(8,128)(2,1)}, u32[]{:S(2)}, u32[]{:S(2)}) %collective-permute-start.14) | collective-permute-done | bytes 262176 | tf_op jit(solution)/shard_map/ppermute | solution.py:49
  137.7 1.0 constant_dynamic-update-slice_fusion.30
  138.6 1.0 constant_dynamic-update-slice_fusion.29
  140.1 1.0 constant_dynamic-update-slice_fusion.15
  141.1 1.0 constant_dynamic-update-slice_fusion.14
  142.1 1.0 constant_dynamic-update-slice_fusion.13
  143.5 3.2 %copy-done.4 = bf16[512,8192]{1,0:T(8,128)(2,1)} copy-done((bf16[512,8192]{1,0:T(8,128)(2,1)}, bf16[512,8192]{1,0:T(8,128)(2,1)S(1)}, u32[]{:S(2)}) %copy-start.4) | copy-done | bytes 8388632
  146.8 7.1 %subtract_convert_fusion = bf16[2,2,256,4096]{3,2,1,0:T(8,128)(2,1)S(1)} fusion(bf16[2,2,256,4096]{3,2,1,0:T(8,128)(2,1)} %param.6, bf16[512,8192]{1,0:T(8,128)(2,1)S(1)} %constant_dynamic-update-slice_fusion, s32[]{:T(128)S(6)} %select_n.14, f32[2,2,512]{2,1,0:T(2,128)S(1)} %get-tuple-element.7, f32[256,512]{1,0:T(8,128)S(1)} %copy-done.3), kind=kOutput, calls=%fused_computation | convolution fusion | flops 4308598784 | bytes 21504004 | tf_op jit(solution)/shard_map/dot_general | solution.py:55
  153.8 3.2 %copy-done = bf16[2,2,256,4096]{3,2,1,0:T(8,128)(2,1)} copy-done((bf16[2,2,256,4096]{3,2,1,0:T(8,128)(2,1)}, bf16[2,2,256,4096]{3,2,1,0:T(8,128)(2,1)S(1)}, u32[]{:S(2)}) %copy-start) | copy-done | bytes 8388632
  157.1 1.3 fusion.5
  158.4 2.9 %fusion.6 = f32[4096,512]{1,0:T(8,128)S(1)} fusion(bf16[256,512]{1,0:T(8,128)(2,1)S(1)} %copy-done.1, bf16[2,2,256,4096]{3,2,1,0:T(8,128)(2,1)} %copy-done), kind=kOutput, calls=%fused_computation.11 | convolution fusion | flops 1073741824 | bytes 10747904 | tf_op jit(solution)/shard_map/dot_general | solution.py:22
  161.3 6.1 %fusion.7 = f32[4096,512]{1,0:T(8,128)} fusion(bf16[256,512]{1,0:T(8,128)(2,1)S(1)} %copy-done.1, bf16[2,2,256,4096]{3,2,1,0:T(8,128)(2,1)} %copy-done), kind=kOutput, calls=%fused_computation.13 | convolution fusion | flops 1073741824 | bytes 10747904 | tf_op jit(solution)/shard_map/dot_general | solution.py:22
  167.4 8.5 %multiply_add_fusion = f32[4096,512]{1,0:T(8,128)} fusion(f32[4096,512]{1,0:T(8,128)S(1)} %fusion.5, f32[4096,512]{1,0:T(8,128)S(1)} %fusion.6, f32[4096,512]{1,0:T(8,128)} %fusion.7, bf16[256,512]{1,0:T(8,128)(2,1)S(1)} %copy-done.1, f32[512]{0:T(512)S(1)} %bitcast.60, f32[512]{0:T(512)S(1)} %bitcast.62, f32[512]{0:T(512)S(1)} %bitcast.64, ...), kind=kOutput, calls=%fused_computation.1 | convolution fusion | flops 1088421888 | bytes 35921920 | tf_op jit(solution)/shard_map/dot_general | solution.py:22
  176.0 8.4 %fusion = f32[2,2,256,512]{3,2,1,0:T(8,128)S(1)} fusion(bf16[2,2,256,4096]{3,2,1,0:T(8,128)(2,1)} %copy-done, bf16[512,8192]{1,0:T(8,128)(2,1)} %copy-done.4, s32[]{:T(128)S(6)} %select_n.14), kind=kOutput, calls=%fused_computation.2 | convolution fusion | flops 4294967296 | bytes 14680068 | tf_op jit(solution)/shard_map/dot_general | solution.py:28
  184.4 1.0 fusion.12
  185.4 91.8 %reduce-scatter.2.cloned.1.call-done = f32[256,512]{1,0:T(8,128)} async-done(((f32[4096,512]{1,0:T(8,128)}), f32[256,512]{1,0:T(8,128)}) %reduce-scatter.2.cloned.1.call-update) | async-done | bytes 524304 | tf_op jit(solution)/shard_map/reduce_scatter | solution.py:73
  277.2 1.9 broadcast_multiply_fusion
  (58 shorter events, 5.3 us)
Async XLA Ops:
  7.2 132.9 %copy-start.2 = (bf16[512,256]{1,0:T(8,128)(2,1)S(1)}, bf16[512,256]{1,0:T(8,128)(2,1)}, u32[]{:S(2)}) copy-start(bf16[512,256]{1,0:T(8,128)(2,1)} %param.8) | copy-start | bytes 786436
  7.2 270.1 %reduce-scatter.2.cloned.1.call-start = ((), (), s32[]{:S(2)}) async-start(), calls=%async_computation.1 | async-start | bytes 8912896 | tf_op jit(solution)/shard_map/reduce_scatter | solution.py:73
  7.2 9.8 %collective-permute-start = (bf16[512,256]{1,0:T(8,128)(2,1)}, bf16[512,256]{1,0:T(8,128)(2,1)S(1)}, u32[]{:S(2)}, u32[]{:S(2)}) collective-permute-start(bf16[512,256]{1,0:T(8,128)(2,1)} %param.8), channel_id=1, source_target_pairs={{0,1},{1,2},{2,3},{3,4},{4,5},{5,6},{6,7},{7,8},{8,9},{9,10},{10,1... | collective-permute-start | bytes 786440 | tf_op jit(solution)/shard_map/ppermute | solution.py:49
  17.0 8.5 %collective-permute-start.1 = (bf16[512,256]{1,0:T(8,128)(2,1)S(1)}, bf16[512,256]{1,0:T(8,128)(2,1)S(1)}, u32[]{:S(2)}, u32[]{:S(2)}) collective-permute-start(bf16[512,256]{1,0:T(8,128)(2,1)S(1)} %collective-permute-done), channel_id=1, source_target_pairs={{0,1},{1,2},{2,3},{3,4},{4,5},{5,6},{6,7},{7,8},{8,9},{9,10},{10,1... | collective-permute-start | bytes 786440 | tf_op jit(solution)/shard_map/ppermute | solution.py:49
  25.5 8.5 %collective-permute-start.2 = (bf16[512,256]{1,0:T(8,128)(2,1)S(1)}, bf16[512,256]{1,0:T(8,128)(2,1)S(1)}, u32[]{:S(2)}, u32[]{:S(2)}) collective-permute-start(bf16[512,256]{1,0:T(8,128)(2,1)S(1)} %collective-permute-done.1), channel_id=1, source_target_pairs={{0,1},{1,2},{2,3},{3,4},{4,5},{5,6},{6,7},{7,8},{8,9},{9,10},{10,1... | collective-permute-start | bytes 786440 | tf_op jit(solution)/shard_map/ppermute | solution.py:49
  34.0 8.5 %collective-permute-start.3 = (bf16[512,256]{1,0:T(8,128)(2,1)S(1)}, bf16[512,256]{1,0:T(8,128)(2,1)S(1)}, u32[]{:S(2)}, u32[]{:S(2)}) collective-permute-start(bf16[512,256]{1,0:T(8,128)(2,1)S(1)} %collective-permute-done.2), channel_id=1, source_target_pairs={{0,1},{1,2},{2,3},{3,4},{4,5},{5,6},{6,7},{7,8},{8,9},{9,10},{10,1... | collective-permute-start | bytes 786440 | tf_op jit(solution)/shard_map/ppermute | solution.py:49
  42.5 8.5 %collective-permute-start.4 = (bf16[512,256]{1,0:T(8,128)(2,1)S(1)}, bf16[512,256]{1,0:T(8,128)(2,1)S(1)}, u32[]{:S(2)}, u32[]{:S(2)}) collective-permute-start(bf16[512,256]{1,0:T(8,128)(2,1)S(1)} %collective-permute-done.3), channel_id=1, source_target_pairs={{0,1},{1,2},{2,3},{3,4},{4,5},{5,6},{6,7},{7,8},{8,9},{9,10},{10,1... | collective-permute-start | bytes 786440 | tf_op jit(solution)/shard_map/ppermute | solution.py:49
  51.0 8.5 %collective-permute-start.5 = (bf16[512,256]{1,0:T(8,128)(2,1)S(1)}, bf16[512,256]{1,0:T(8,128)(2,1)S(1)}, u32[]{:S(2)}, u32[]{:S(2)}) collective-permute-start(bf16[512,256]{1,0:T(8,128)(2,1)S(1)} %collective-permute-done.4), channel_id=1, source_target_pairs={{0,1},{1,2},{2,3},{3,4},{4,5},{5,6},{6,7},{7,8},{8,9},{9,10},{10,1... | collective-permute-start | bytes 786440 | tf_op jit(solution)/shard_map/ppermute | solution.py:49
  59.5 8.5 %collective-permute-start.6 = (bf16[512,256]{1,0:T(8,128)(2,1)S(1)}, bf16[512,256]{1,0:T(8,128)(2,1)S(1)}, u32[]{:S(2)}, u32[]{:S(2)}) collective-permute-start(bf16[512,256]{1,0:T(8,128)(2,1)S(1)} %collective-permute-done.5), channel_id=1, source_target_pairs={{0,1},{1,2},{2,3},{3,4},{4,5},{5,6},{6,7},{7,8},{8,9},{9,10},{10,1... | collective-permute-start | bytes 786440 | tf_op jit(solution)/shard_map/ppermute | solution.py:49
  68.0 8.5 %collective-permute-start.7 = (bf16[512,256]{1,0:T(8,128)(2,1)S(1)}, bf16[512,256]{1,0:T(8,128)(2,1)S(1)}, u32[]{:S(2)}, u32[]{:S(2)}) collective-permute-start(bf16[512,256]{1,0:T(8,128)(2,1)S(1)} %collective-permute-done.6), channel_id=1, source_target_pairs={{0,1},{1,2},{2,3},{3,4},{4,5},{5,6},{6,7},{7,8},{8,9},{9,10},{10,1... | collective-permute-start | bytes 786440 | tf_op jit(solution)/shard_map/ppermute | solution.py:49
  76.5 8.5 %collective-permute-start.8 = (bf16[512,256]{1,0:T(8,128)(2,1)S(1)}, bf16[512,256]{1,0:T(8,128)(2,1)S(1)}, u32[]{:S(2)}, u32[]{:S(2)}) collective-permute-start(bf16[512,256]{1,0:T(8,128)(2,1)S(1)} %collective-permute-done.7), channel_id=1, source_target_pairs={{0,1},{1,2},{2,3},{3,4},{4,5},{5,6},{6,7},{7,8},{8,9},{9,10},{10,1... | collective-permute-start | bytes 786440 | tf_op jit(solution)/shard_map/ppermute | solution.py:49
  85.0 8.5 %collective-permute-start.9 = (bf16[512,256]{1,0:T(8,128)(2,1)S(1)}, bf16[512,256]{1,0:T(8,128)(2,1)S(1)}, u32[]{:S(2)}, u32[]{:S(2)}) collective-permute-start(bf16[512,256]{1,0:T(8,128)(2,1)S(1)} %collective-permute-done.8), channel_id=1, source_target_pairs={{0,1},{1,2},{2,3},{3,4},{4,5},{5,6},{6,7},{7,8},{8,9},{9,10},{10,1... | collective-permute-start | bytes 786440 | tf_op jit(solution)/shard_map/ppermute | solution.py:49
  93.5 8.5 %collective-permute-start.10 = (bf16[512,256]{1,0:T(8,128)(2,1)S(1)}, bf16[512,256]{1,0:T(8,128)(2,1)S(1)}, u32[]{:S(2)}, u32[]{:S(2)}) collective-permute-start(bf16[512,256]{1,0:T(8,128)(2,1)S(1)} %collective-permute-done.9), channel_id=1, source_target_pairs={{0,1},{1,2},{2,3},{3,4},{4,5},{5,6},{6,7},{7,8},{8,9},{9,10},{10,1... | collective-permute-start | bytes 786440 | tf_op jit(solution)/shard_map/ppermute | solution.py:49
  102.0 8.5 %collective-permute-start.11 = (bf16[512,256]{1,0:T(8,128)(2,1)S(1)}, bf16[512,256]{1,0:T(8,128)(2,1)S(1)}, u32[]{:S(2)}, u32[]{:S(2)}) collective-permute-start(bf16[512,256]{1,0:T(8,128)(2,1)S(1)} %collective-permute-done.10), channel_id=1, source_target_pairs={{0,1},{1,2},{2,3},{3,4},{4,5},{5,6},{6,7},{7,8},{8,9},{9,10},{10,1... | collective-permute-start | bytes 786440 | tf_op jit(solution)/shard_map/ppermute | solution.py:49
  110.5 8.6 %collective-permute-start.12 = (bf16[512,256]{1,0:T(8,128)(2,1)S(1)}, bf16[512,256]{1,0:T(8,128)(2,1)}, u32[]{:S(2)}, u32[]{:S(2)}) collective-permute-start(bf16[512,256]{1,0:T(8,128)(2,1)S(1)} %collective-permute-done.11), channel_id=1, source_target_pairs={{0,1},{1,2},{2,3},{3,4},{4,5},{5,6},{6,7},{7,8},{8,9},{9,10},{10,1... | collective-permute-start | bytes 786440 | tf_op jit(solution)/shard_map/ppermute | solution.py:49
  119.1 8.8 %collective-permute-start.13 = (bf16[512,256]{1,0:T(8,128)(2,1)}, bf16[512,256]{1,0:T(8,128)(2,1)}, u32[]{:S(2)}, u32[]{:S(2)}) collective-permute-start(bf16[512,256]{1,0:T(8,128)(2,1)} %collective-permute-done.12), channel_id=1, source_target_pairs={{0,1},{1,2},{2,3},{3,4},{4,5},{5,6},{6,7},{7,8},{8,9},{9,10},{10,1... | collective-permute-start | bytes 786440 | tf_op jit(solution)/shard_map/ppermute | solution.py:49
  127.9 8.8 %collective-permute-start.14 = (bf16[512,256]{1,0:T(8,128)(2,1)}, bf16[512,256]{1,0:T(8,128)(2,1)}, u32[]{:S(2)}, u32[]{:S(2)}) collective-permute-start(bf16[512,256]{1,0:T(8,128)(2,1)} %collective-permute-done.13), channel_id=1, source_target_pairs={{0,1},{1,2},{2,3},{3,4},{4,5},{5,6},{6,7},{7,8},{8,9},{9,10},{10,1... | collective-permute-start | bytes 786440 | tf_op jit(solution)/shard_map/ppermute | solution.py:49
  129.8 17.0 %copy-start.3 = (f32[256,512]{1,0:T(8,128)S(1)}, f32[256,512]{1,0:T(8,128)}, u32[]{:S(2)}) copy-start(f32[256,512]{1,0:T(8,128)} %convert_element_type.22) | copy-start | bytes 1572868
  143.5 3.2 %copy-start.4 = (bf16[512,8192]{1,0:T(8,128)(2,1)}, bf16[512,8192]{1,0:T(8,128)(2,1)S(1)}, u32[]{:S(2)}) copy-start(bf16[512,8192]{1,0:T(8,128)(2,1)S(1)} %constant_dynamic-update-slice_fusion) | copy-start | bytes 25165828
  146.8 10.3 %copy-start.1 = (bf16[256,512]{1,0:T(8,128)(2,1)S(1)}, bf16[256,512]{1,0:T(8,128)(2,1)}, u32[]{:S(2)}) copy-start(bf16[256,512]{1,0:T(8,128)(2,1)} %param.7) | copy-start | bytes 786436
  153.8 3.2 %copy-start = (bf16[2,2,256,4096]{3,2,1,0:T(8,128)(2,1)}, bf16[2,2,256,4096]{3,2,1,0:T(8,128)(2,1)S(1)}, u32[]{:S(2)}) copy-start(bf16[2,2,256,4096]{3,2,1,0:T(8,128)(2,1)S(1)} %subtract_convert_fusion) | copy-start | bytes 25165828
Sparse Core Ops, SparseCore 0:
  176.1 101.1 reduce-scatter.1
